TPU v7x, 256 devices: a whole 4x4x8 slice. The times are simulated.
256 devices in a mesh: dp: 32 (over z, x_hi, core), seq: 8 (over y, x_lo).
Axes of the slice: x: 4 (x_hi: 2, x_lo: 2; x = x_hi * 2 + x_lo), y: 4, z: 8, core: 2. Of those that a mesh axis runs over, the one named last changes fastest.
Arguments:
- grad_out: bfloat16 [32, 1024, 6144], P('dp', 'seq'), may hold values from -6 to 6
- queries: bfloat16 [32, 1024, 3072], P('dp', 'seq'), may hold values from -40 to 40
- keys: bfloat16 [32, 1024, 3072], P('dp', 'seq'), may hold values from -12 to 12
- values: bfloat16 [32, 1024, 3072], P('dp', 'seq'), may hold values from -6 to 6
- out_weight: bfloat16 [6144, 3072], P('dp', 'seq'), may hold values from -0.109375 to 0.109375
Outputs:
- query_grad: bfloat16 [32, 1024, 3072], P('dp', 'seq')
- key_grad: bfloat16 [32, 1024, 3072], P('dp', 'seq')
- value_grad: bfloat16 [32, 1024, 3072], P('dp', 'seq')
- weight_grad: float32 [6144, 3072], P('dp', 'seq')
All inputs are finite; a program needn't handle non-finite values.
Results may differ from a plain program's by a relative error of at most 0.03.
Values may be sent and summed in bfloat16 or wider, within the bound.
A program may use at most 128 MiB of HBM per device.

v0:
```python
import math

import jax
import jax.numpy as jnp
from jax import lax
from jax.sharding import PartitionSpec as P

HEAD_DIM = 128


def shards(grad_out, queries, keys, values, out_weight):
    gathered = lax.all_gather(grad_out, "seq", axis=1, tiled=True)[0]
    length = gathered.shape[0]
    features = out_weight.shape[1]
    heads_here = features // HEAD_DIM
    whole_rows = lax.all_gather(out_weight, "dp", axis=0, tiled=True)
    d_full = jnp.dot(gathered, whole_rows, preferred_element_type=jnp.float32)
    d_attn = d_full.astype(jnp.bfloat16)
    query_all, key_all, value_all = (
        lax.all_to_all(queries, "seq", split_axis=2, concat_axis=1, tiled=True),
        lax.all_to_all(keys, "seq", split_axis=2, concat_axis=1, tiled=True),
        lax.all_to_all(values, "seq", split_axis=2, concat_axis=1, tiled=True),
    )
    head_shape = (length, heads_here, HEAD_DIM)
    query_heads = query_all[0].reshape(head_shape)
    key_heads = key_all[0].reshape(head_shape)
    value_heads = value_all[0].reshape(head_shape)
    grad_heads = d_attn.reshape(head_shape)
    block_rows = math.gcd(length, 512)
    block_count = length // block_rows
    block_shape = (block_count, block_rows, heads_here, HEAD_DIM)
    query_blocks = query_heads.reshape(block_shape)
    grad_blocks = grad_heads.reshape(block_shape)
    inverse_root = 1.0 / math.sqrt(HEAD_DIM)
    token_scale = 1.0 / math.sqrt(lax.axis_size("dp") * length)

    def softmax_rows(query_block):
        scores = (
            jnp.einsum("qhd,khd->hqk", query_block, key_heads, preferred_element_type=jnp.float32)
            * inverse_root
        )
        largest = jnp.max(scores, axis=-1, keepdims=True)
        raised = jnp.exp(scores - largest)
        probabilities = raised / jnp.sum(raised, axis=-1, keepdims=True)
        return (probabilities, probabilities.astype(jnp.bfloat16))

    def attend(probs_low):
        return jnp.einsum(
            "hqk,khd->qhd", probs_low, value_heads, preferred_element_type=jnp.float32
        ).astype(jnp.bfloat16)

    def backward(totals, probabilities, probs_low, attended, query_block, grad_block):
        key_sums, value_sums = totals
        value_sums = value_sums + jnp.einsum(
            "hqk,qhd->khd", probs_low, grad_block, preferred_element_type=jnp.float32
        )
        d_probs = jnp.einsum(
            "qhd,khd->hqk", grad_block, value_heads, preferred_element_type=jnp.float32
        )
        row_delta = jnp.sum(grad_block.astype(jnp.float32) * attended.astype(jnp.float32), axis=-1)
        d_scores = probabilities * (d_probs - jnp.transpose(row_delta)[:, :, None])
        scores_low = d_scores.astype(jnp.bfloat16)
        query_part = (
            jnp.einsum("hqk,khd->qhd", scores_low, key_heads, preferred_element_type=jnp.float32)
            * inverse_root
        ).astype(jnp.bfloat16)
        key_sums = key_sums + jnp.einsum(
            "hqk,qhd->khd", scores_low, query_block, preferred_element_type=jnp.float32
        )
        return ((key_sums, value_sums), query_part)

    zero_sums = (jnp.zeros(head_shape, jnp.float32), jnp.zeros(head_shape, jnp.float32))

    def advance(totals, pieces):
        query_block, grad_block = pieces
        probabilities, probs_low = softmax_rows(query_block)
        attended = attend(probs_low)
        totals, query_part = backward(
            totals, probabilities, probs_low, attended, query_block, grad_block
        )
        return (totals, (query_part, attended))

    (key_sums, value_sums), (query_parts, attended_blocks) = lax.scan(
        advance, zero_sums, (query_blocks, grad_blocks)
    )
    attended_all = attended_blocks.reshape(length, features)
    product = lax.dot_general(
        gathered, attended_all, (((0,), (0,)), ((), ())), preferred_element_type=jnp.float32
    )
    weight_grad = lax.psum_scatter(
        (product * token_scale).astype(jnp.bfloat16), "dp", scatter_dimension=0, tiled=True
    ).astype(jnp.float32)
    query_local = query_parts.reshape(1, length, features)
    key_local = (key_sums * inverse_root).astype(jnp.bfloat16).reshape(1, length, features)
    value_local = value_sums.astype(jnp.bfloat16).reshape(1, length, features)
    query_grad, key_grad, value_grad = (
        lax.all_to_all(query_local, "seq", split_axis=1, concat_axis=2, tiled=True),
        lax.all_to_all(key_local, "seq", split_axis=1, concat_axis=2, tiled=True),
        lax.all_to_all(value_local, "seq", split_axis=1, concat_axis=2, tiled=True),
    )
    return (query_grad, key_grad, value_grad, weight_grad)


def solution(mesh):
    in_specs = (
        P("dp", "seq", None),
        P("dp", "seq", None),
        P("dp", "seq", None),
        P("dp", "seq", None),
        P("dp", "seq"),
    )
    out_specs = (P("dp", "seq", None), P("dp", "seq", None), P("dp", "seq", None), P("dp", "seq"))
    return jax.shard_map(shards, mesh=mesh, in_specs=in_specs, out_specs=out_specs, check_vma=False)
```

profile of v0, /device:TPU:6, one launch (start us, length us, event | category | flops | bytes accessed | tf_op | source)
XLA Modules:
  0.0 577.3 jit_solution(2107303295354958740)
XLA Ops:
  8.6 3.7 copy.111
  12.8 16.9 %reduce = bf16[3072,128]{1,0:T(8,128)(2,1)S(1)} reduce(bf16[3072,1,128]{2,1,0:T(2,128)(2,1)S(1)} %bitcast.154, bf16[]{:T(256)} %broadcast.43), dimensions={1}, to_apply=%bitcast.87.reduce_sub_computation | reduce | bytes 1572866
  29.7 1.1 reshape.34
  30.7 5.9 %all-to-all-start = ((bf16[8,2,24576]{2,1,0:T(2,128)(2,1)}), bf16[8,2,24576]{2,1,0:T(2,128)(2,1)S(1)}, u32[]{:S(2)}, u32[]{:S(2)}) async-start(bf16[8,2,24576]{2,1,0:T(2,128)(2,1)} %reshape.34), calls=%async_computation | async-start | bytes 1572864 | tf_op jit(solution)/shard_map/all_to_all | solution.py:20
  36.7 3.7 copy.113
  40.4 16.9 %reduce.1 = bf16[3072,128]{1,0:T(8,128)(2,1)S(1)} reduce(bf16[3072,1,128]{2,1,0:T(2,128)(2,1)S(1)} %bitcast.164, bf16[]{:T(256)} %broadcast.43), dimensions={1}, to_apply=%bitcast.89.reduce_sub_computation | reduce | bytes 1572866
  57.2 1.1 reshape.36
  58.3 6.2 %all-to-all-start.1 = ((bf16[8,2,24576]{2,1,0:T(2,128)(2,1)}), bf16[8,2,24576]{2,1,0:T(2,128)(2,1)}, u32[]{:S(2)}, u32[]{:S(2)}) async-start(bf16[8,2,24576]{2,1,0:T(2,128)(2,1)} %reshape.36), calls=%async_computation.1 | async-start | bytes 1572864 | tf_op jit(solution)/shard_map/all_to_all | solution.py:21
  64.5 3.7 copy.116
  68.2 16.9 %reduce.2 = bf16[3072,128]{1,0:T(8,128)(2,1)S(1)} reduce(bf16[3072,1,128]{2,1,0:T(2,128)(2,1)S(1)} %bitcast.165, bf16[]{:T(256)} %broadcast.43), dimensions={1}, to_apply=%bitcast.91.reduce_sub_computation | reduce | bytes 1572866
  85.1 1.1 reshape.38
  86.1 5.7 all-to-all-start.2
  91.9 5.5 reshape.35
  97.4 1.5 copy.143
  98.9 1.4 copy.112
  100.3 2.7 reshape_reshape_squeeze.3
  103.0 3.1 copy.118
  106.1 5.5 reshape.37
  111.6 1.5 copy.144
  113.1 1.4 copy.114
  114.5 2.2 reshape_squeeze.6
  116.7 2.3 copy.119
  119.0 5.6 reshape.39
  124.5 1.5 copy.145
  126.1 1.4 copy.117
  127.5 2.2 reshape_squeeze.7
  129.6 229.7 %all-gather.3.cloned.1.call-done = bf16[1,1024,6144]{2,1,0:T(8,128)(2,1)} async-done(((bf16[1,128,6144]{2,1,0:T(8,128)(2,1)}), bf16[1,1024,6144]{2,1,0:T(8,128)(2,1)}) %all-gather.3.cloned.1.call-update) | async-done | bytes 12582928 | tf_op jit(solution)/shard_map/all_gather | solution.py:12
  359.3 11.7 %fusion.45 = bf16[1024,384]{1,0:T(8,128)(2,1)} fusion(bf16[6144,384]{1,0:T(8,128)(2,1)} %all-gather.5.cloned.1.call-done, bf16[1,1024,6144]{2,1,0:T(8,128)(2,1)} %all-gather.3.cloned.1.call-done), kind=kOutput, calls=%fused_computation.42 | convolution fusion | flops 4832231424 | bytes 18087936 | tf_op jit(solution)/shard_map/dot_general | solution.py:17
  371.1 3.2 reshape.30
  374.3 2.2 copy.120
  376.6 35.0 %while.17 = (s32[]{:T(128)}, f32[1024,3,128]{0,2,1:T(8,128)S(1)}, f32[1024,3,128]{0,2,1:T(8,128)S(1)}, bf16[2,512,3,128]{3,1,2,0:T(8,128)(2,1)}, bf16[2,512,3,12...) while((s32[]{:T(128)}, f32[1024,3,128]{0,2,1:T(8,128)S(1)}, ...), condition=%wide.region_4.5_spmd.clone, body=%wide.region_0.4_spmd.clone.sunk | while | flops 2433023488 | bytes 94800312 | solution.py:83
  376.7 5.8 %fusion.91 = (f32[3,512]{1,0:T(4,128)S(1)}, f32[3,512,1024]{2,1,0:T(8,128)}) fusion(bf16[1024,3,128]{2,0,1:T(8,128)(2,1)} %get-tuple-element.279, bf16[2,512,3,128]{3,1,2,0:T(8,128)(2,1)} %get-tuple-element.278, s32[]{:T(128)S(6)} %copy.157), kind=kOutput, calls=%fused_computation.43.clone.1 | convolution fusion | flops 407372800 | bytes 7477252 | tf_op jit(solution)/shard_map/while/body/eval_jaxpr/sub | solution.py:43
  382.5 3.6 fusion.92
  386.2 1.1 multiply_reduce_fusion.3
  389.3 1.2 multiply_convert_fusion.4
  390.6 1.1 fusion.93
  394.1 5.8 %fusion.91 = (f32[3,512]{1,0:T(4,128)S(1)}, f32[3,512,1024]{2,1,0:T(8,128)}) fusion(bf16[1024,3,128]{2,0,1:T(8,128)(2,1)} %get-tuple-element.279, bf16[2,512,3,128]{3,1,2,0:T(8,128)(2,1)} %get-tuple-element.278, s32[]{:T(128)S(6)} %copy.157), kind=kOutput, calls=%fused_computation.43.clone.1 | convolution fusion | flops 407372800 | bytes 7477252 | tf_op jit(solution)/shard_map/while/body/eval_jaxpr/sub | solution.py:43
  400.0 3.6 fusion.92
  403.6 1.1 multiply_reduce_fusion.3
  406.7 1.2 multiply_convert_fusion.4
  408.1 1.1 fusion.93
  411.6 3.0 copy.128
  414.6 1.3 copy.149
  415.9 11.3 %fusion.42 = bf16[6144,384]{0,1:T(8,128)(2,1)} fusion(bf16[1024,384]{0,1:T(8,128)(2,1)S(1)} %bitcast.178, bf16[1,1024,6144]{2,1,0:T(8,128)(2,1)} %all-gather.3.cloned.1.call-done), kind=kOutput, calls=%fused_computation.40 | convolution fusion | flops 4836556800 | bytes 18087936 | tf_op jit(solution)/shard_map/dot_general | solution.py:87
  427.2 6.6 %copy.140 = bf16[6144,384]{1,0:T(8,128)(2,1)} copy(bf16[6144,384]{0,1:T(8,128)(2,1)} %fusion.42) | data formatting | bytes 9437184
  434.9 4.3 copy.124
  439.2 6.2 %reduce.4 = bf16[1024,384]{1,0:T(8,128)(2,1)} reduce(bf16[1024,1,384]{2,1,0:T(2,128)(2,1)S(1)} %bitcast.159, bf16[]{:T(256)} %broadcast.43), dimensions={1}, to_apply=%bitcast.95.reduce_sub_computation | reduce | bytes 1572866
  445.5 2.8 reshape.42
  448.3 5.5 all-to-all-start.4
  453.9 2.2 copy.126
  456.1 5.3 reduce.5
  461.4 1.1 reshape.44
  462.5 3.0 all-to-all-done.4
  465.5 5.3 all-to-all-start.5
  472.2 5.3 reduce.3
  477.6 1.1 reshape.40
  478.7 2.7 all-to-all-done.5
  481.4 4.7 all-to-all-start.3
  487.4 1.2 copy.130
  488.6 4.1 reshape.45
  493.2 1.2 copy.131
  494.4 6.8 %all-to-all-done.3 = bf16[8,2,24576]{2,1,0:T(2,128)(2,1)S(1)} async-done(((bf16[8,2,24576]{2,1,0:T(2,128)(2,1)}), bf16[8,2,24576]{2,1,0:T(2,128)(2,1)S(1)}, u32[]{:S(2)}, u32[]{:S(2)}) %all-to-all-start.3) | async-done | bytes 786464 | tf_op jit(solution)/shard_map/all_to_all | solution.py:97
  502.5 1.2 copy.129
  503.6 64.8 %reduce-scatter.4.cloned.1.call-done = bf16[192,384]{1,0:T(8,128)(2,1)} async-done(((bf16[6144,384]{1,0:T(8,128)(2,1)}), bf16[192,384]{1,0:T(8,128)(2,1)}) %reduce-scatter.4.cloned.1.call-update) | async-done | bytes 147472
  (81 shorter events, 18.6 us)
Async XLA Ops:
  7.2 122.5 %all-gather.5.cloned.1.call-start = ((), (), s32[]{:S(2)}) async-start(), calls=%async_computation.8 | async-start | bytes 4866048 | tf_op jit(solution)/shard_map/all_gather | solution.py:16
  7.9 351.4 %all-gather.3.cloned.1.call-start = ((), (), s32[]{:S(2)}) async-start(), calls=%async_computation.7 | async-start | bytes 14155776 | tf_op jit(solution)/shard_map/all_gather | solution.py:12
  30.7 27.5 %all-to-all-start = ((bf16[8,2,24576]{2,1,0:T(2,128)(2,1)}), bf16[8,2,24576]{2,1,0:T(2,128)(2,1)S(1)}, u32[]{:S(2)}, u32[]{:S(2)}) async-start(bf16[8,2,24576]{2,1,0:T(2,128)(2,1)} %reshape.34), calls=%async_computation | async-start | bytes 1572864 | tf_op jit(solution)/shard_map/all_to_all | solution.py:20
  58.3 26.8 %copy-start.2 = (bf16[8,2,24576]{2,1,0:T(2,128)(2,1)}, bf16[8,2,24576]{2,1,0:T(2,128)(2,1)S(1)}, u32[]{:S(2)}) copy-start(bf16[8,2,24576]{2,1,0:T(2,128)(2,1)S(1)} %all-to-all-done) | copy-start | bytes 2359300
  58.3 27.9 %all-to-all-start.1 = ((bf16[8,2,24576]{2,1,0:T(2,128)(2,1)}), bf16[8,2,24576]{2,1,0:T(2,128)(2,1)}, u32[]{:S(2)}, u32[]{:S(2)}) async-start(bf16[8,2,24576]{2,1,0:T(2,128)(2,1)} %reshape.36), calls=%async_computation.1 | async-start | bytes 1572864 | tf_op jit(solution)/shard_map/all_to_all | solution.py:21
  86.1 32.9 %all-to-all-start.2 = ((bf16[8,2,24576]{2,1,0:T(2,128)(2,1)}), bf16[8,2,24576]{2,1,0:T(2,128)(2,1)}, u32[]{:S(2)}, u32[]{:S(2)}) async-start(bf16[8,2,24576]{2,1,0:T(2,128)(2,1)} %reshape.38), calls=%async_computation.2 | async-start | bytes 1572864 | tf_op jit(solution)/shard_map/all_to_all | solution.py:22
  91.8 476.6 %reduce-scatter.4.cloned.1.call-start = ((), (), s32[]{:S(2)}) async-start(), calls=%async_computation.9 | async-start | bytes 4866048
  382.5 3.6 copy-start.1
  382.5 3.6 copy-start.7
  386.2 2.2 slice-start
  387.3 2.0 slice-start.1
  389.3 1.2 copy-start.3
  389.3 1.4 copy-start.6
  390.6 1.1 copy-start
  391.8 1.0 copy-start.4
  391.8 1.4 copy-start.8
  393.3 0.9 copy-start.9
  399.9 3.6 copy-start.1
  399.9 3.6 copy-start.7
  403.6 2.2 slice-start
  404.7 2.0 slice-start.1
  406.7 1.2 copy-start.3
  406.7 1.4 copy-start.6
  408.1 1.1 copy-start
  409.2 1.0 copy-start.4
  409.2 1.4 copy-start.8
  410.7 0.9 copy-start.9
  448.3 17.2 %all-to-all-start.4 = ((bf16[8,2,24576]{2,1,0:T(2,128)(2,1)}), bf16[8,2,24576]{2,1,0:T(2,128)(2,1)S(1)}, u32[]{:S(2)}, u32[]{:S(2)}) async-start(bf16[8,2,24576]{2,1,0:T(2,128)(2,1)} %reshape.42), calls=%async_computation.4 | async-start | bytes 1572864 | tf_op jit(solution)/shard_map/all_to_all | solution.py:98
  461.4 9.3 %copy-start.5 = (bf16[2,512,3,128]{3,1,2,0:T(8,128)(2,1)S(1)}, bf16[2,512,3,128]{3,1,2,0:T(8,128)(2,1)}, u32[]{:S(2)}) copy-start(bf16[2,512,3,128]{3,1,2,0:T(8,128)(2,1)} %get-tuple-element.54) | copy-start | bytes 2359300
  465.5 15.9 %all-to-all-start.5 = ((bf16[8,2,24576]{2,1,0:T(2,128)(2,1)}), bf16[8,2,24576]{2,1,0:T(2,128)(2,1)}, u32[]{:S(2)}, u32[]{:S(2)}) async-start(bf16[8,2,24576]{2,1,0:T(2,128)(2,1)} %reshape.44), calls=%async_computation.5 | async-start | bytes 1572864 | tf_op jit(solution)/shard_map/all_to_all | solution.py:99
  481.4 19.8 %all-to-all-start.3 = ((bf16[8,2,24576]{2,1,0:T(2,128)(2,1)}), bf16[8,2,24576]{2,1,0:T(2,128)(2,1)S(1)}, u32[]{:S(2)}, u32[]{:S(2)}) async-start(bf16[8,2,24576]{2,1,0:T(2,128)(2,1)} %reshape.40), calls=%async_computation.3 | async-start | bytes 1572864 | tf_op jit(solution)/shard_map/all_to_all | solution.py:97
Sparse Core Ops, SparseCore 0:
  10.8 98.6 all-gather.4
  111.2 248.0 all-gather.2
  434.0 134.4 reduce-scatter.3
where the time goes:
time: 589 us; the launch traced here: 577 us
  waiting for transfers between devices  308 us (52%)
  local copies, waits for them, and re-layouts  99.6 us (17%)
  other arithmetic  75.8 us (13%)
  matrix products  45.4 us (8%)
  starting transfers between devices  33.4 us (6%)
  between operations  14.4 us (2%)
    all_gather x1, waiting for transfers between devices, shards(): gathered = lax.all_gather(grad_out, 'seq', axis=1, tiled=True)[0]  230 us
    unnamed x36, local copies, waits for them, and re-layouts  67.8 us
    unnamed x8, other arithmetic  67.5 us
    unnamed x4, waiting for transfers between devices  66.2 us
  transfers between devices with their start and end apart: 9, of which 5 were waited for; matrix products, arithmetic and copies ran while one was open for 25% of the time, Pallas kernels for 0%

commit v1 on v0

v1 whole, which is shorter than its diff:
```python
import math

import jax
import jax.numpy as jnp
from jax import lax
from jax.experimental import pallas as pl
from jax.experimental.pallas import tpu as pltpu
from jax.sharding import PartitionSpec as P

HEAD_DIM = 128
MESH = pl.DeviceIdType.MESH
F32 = jnp.float32
BF16 = jnp.bfloat16
NZ, NY = 8, 4
NT = (((1,), (1,)), ((), ()))
TN = (((0,), (0,)), ((), ()))


def dot(a, b):
    return jnp.dot(a, b, preferred_element_type=F32)


def make_kernel(tokens, model, wide, rows, cols, clips):
    heads = cols // HEAD_DIM
    length = tokens * 8
    half = length // 2
    strip = 2 * rows
    pair = 2 * cols
    deep = NZ * strip
    inverse_root = 1.0 / math.sqrt(HEAD_DIM)
    power = inverse_root * math.log2(math.e)
    token_scale = 1.0 / math.sqrt(clips * length)
    block = 256
    blocks = length // block

    def kernel(
        g_in, q_in, k_in, v_in, w_in,
        dq_out, dk_out, dv_out, wg_out,
        gb, wb, qb, kb, vb, pt, dsb, kt, vt, ot, att, acat, dob, dsend, dacc,
        pb, rc, rr, fx, xr, dqb, dkb, dvb,
        loc, wx_s, wx_r, wz_s, wz_r, wc_s, wc_r, qkv_s, qkv_r, g_s, g_r,
        ex_s, ex_r, pc_s, pc_r, rr_s, rr_r, x_s, x_r, gr_s, gr_r,
    ):
        dp = lax.axis_index("dp")
        seq = lax.axis_index("seq")
        z, xh, c = dp // 4, (dp // 2) % 2, dp % 2
        y, xl = seq // 2, seq % 2

        def seq_peer(dy, b):
            return {"dp": dp, "seq": ((y + dy) % NY) * 2 + (xl + b) % 2}

        def x_peer(a, b):
            return {"dp": z * 4 + ((xh + a) % 2) * 2 + c, "seq": y * 2 + (xl + b) % 2}

        def z_peer(dz):
            return {"dp": ((z + dz + NZ) % NZ) * 4 + xh * 2 + c, "seq": seq}

        core_peer = {"dp": z * 4 + xh * 2 + (1 - c), "seq": seq}
        seq_offsets = [(dy, b) for dy in range(NY) for b in range(2) if dy or b]
        x_offsets = [(0, 1), (1, 1), (1, 0)]

        def remote(src, dst, send, recv, device):
            copy = pltpu.make_async_remote_copy(
                src_ref=src, dst_ref=dst, send_sem=send, recv_sem=recv,
                device_id=device, device_id_type=MESH,
            )
            copy.start()
            return copy

        barrier = pltpu.get_barrier_semaphore()
        partners = [seq_peer(*o) for o in seq_offsets] + [core_peer, z_peer(1), z_peer(-1)]
        partners += [x_peer(1, 0), x_peer(1, 1)]
        for device in partners:
            pl.semaphore_signal(barrier, inc=1, device_id=device, device_id_type=MESH)

        def w_rows(zz, cc):
            return pl.ds(pl.multiple_of(zz * strip + cc * rows, 64), rows)

        def col(i, width):
            return pl.ds(pl.multiple_of(i * width, 128), width)

        own_rows = pl.ds(pl.multiple_of(xl * half + y * tokens, 128), tokens)
        y_rows = pl.ds(pl.multiple_of(y * tokens, 128), tokens)
        local = [
            pltpu.make_async_copy(
                w_in, wb.at[xh, w_rows(z, c), col(xl, cols)], loc.at[0]
            )
        ]
        for t, (src, dst) in enumerate(((q_in, qb), (k_in, kb), (v_in, vb))):
            local.append(
                pltpu.make_async_copy(src.at[:, col(seq, cols)], dst.at[own_rows, :], loc.at[1 + t])
            )
        for s in range(2):
            for zz in range(NZ):
                local.append(
                    pltpu.make_async_copy(
                        g_in.at[:, pl.ds((2 * zz + s) * strip, strip)],
                        gb.at[s, y_rows, pl.ds(zz * strip, strip)],
                        loc.at[4 + s * NZ + zz],
                    )
                )
        for copy in local:
            copy.start()
        pl.semaphore_wait(barrier, len(partners))

        wx = [
            remote(
                w_in, wb.at[xh, w_rows(z, c), col(xl, cols)], wx_s.at[i], wx_r.at[i], x_peer(a, b)
            )
            for i, (a, b) in enumerate(x_offsets)
        ]
        qkv = []
        for i, (dy, b) in enumerate(seq_offsets):
            device = seq_peer(dy, b)
            for t, (src, dst) in enumerate(((q_in, qb), (k_in, kb), (v_in, vb))):
                qkv.append(
                    remote(
                        src.at[:, col(device["seq"], cols)], dst.at[own_rows, :],
                        qkv_s.at[i, t], qkv_r.at[i, t], device,
                    )
                )
        for copy in local:
            copy.wait()
        for copy in wx:
            copy.wait_recv()

        wz = {}
        wc = []

        def w_block(s, zz, cc):
            return wb.at[s, w_rows(zz, cc), :]

        def w_core(s, zz, slot):
            wc.append(
                remote(w_block(s, zz, c), w_block(s, zz, c), wc_s.at[s, slot], wc_r.at[s, slot], core_peer)
            )

        def w_send(d, s, j):
            zz = (z - j + NZ) % NZ if d == 0 else (z + j) % NZ
            ref = w_block(s, zz, c)
            wz[d, s, j] = remote(ref, ref, wz_s.at[d, s, j], wz_r.at[d, s, j], z_peer(1 if d == 0 else -1))

        def w_steps(d, s):
            return 4 if d == s else 3

        for s in range(2):
            for d in range(2):
                w_send(d, s, 0)
        for s in range(2):
            w_core(s, z, 0)
        for j in range(4):
            for s in range(2):
                for d in range(2):
                    if j < w_steps(d, s):
                        wz[d, s, j].wait_recv()
                        if j + 1 < w_steps(d, s):
                            w_send(d, s, j + 1)
                        zz = (z - 1 - j + NZ) % NZ if d == 0 else (z + 1 + j) % NZ
                        w_core(s, zz, 1 + 2 * j + d if j < 3 else 7)

        g = {}
        for s in range(2):
            for dy in (1, 3, 2):
                for zz in range(NZ):
                    g[s, dy, zz] = remote(
                        g_in.at[:, pl.ds((2 * zz + s) * strip, strip)],
                        gb.at[s, y_rows, pl.ds(zz * strip, strip)],
                        g_s.at[s, dy - 1, zz], g_r.at[s, dy - 1, zz], seq_peer(dy, 0),
                    )

        for copy in qkv:
            copy.wait_recv()

        for h in range(heads):
            hc = pl.ds(h * HEAD_DIM, HEAD_DIM)
            kt[h] = jnp.transpose(kb[:, hc].astype(F32)).astype(BF16)
            vt[h] = jnp.transpose(vb[:, hc].astype(F32)).astype(BF16)

            @pl.loop(0, blocks)
            def _(i):
                at = pl.ds(pl.multiple_of(i * block, block), block)
                scores = lax.dot_general(kb[:, hc], qb[at, hc], NT, preferred_element_type=F32)
                largest = jnp.max(scores, axis=0, keepdims=True)
                raised = jnp.exp2((scores - largest) * power)
                total = jnp.sum(raised, axis=0, keepdims=True)
                low = (raised * (1.0 / total)).astype(BF16)
                pt[h, :, at] = low
                out = dot(vt[h], low).astype(BF16)
                ot[h, :, at] = out
                att[at, hc] = jnp.transpose(out.astype(F32)).astype(BF16)

        mine = pl.ds(pl.multiple_of(xl * half, 128), half)
        theirs = pl.ds(pl.multiple_of((1 - xl) * half, 128), half)
        x_partner = seq_peer(0, 1)
        att_copy = remote(
            att.at[theirs, :], acat.at[:, col(xl, cols)], ex_s.at[0], ex_r.at[0], x_partner
        )
        acat[:, col(xl, cols)] = att[mine, :]
        att_copy.wait_recv()
        for copy in wc:
            copy.wait_recv()

        def project(s):
            chunk = deep // 4

            @pl.loop(0, 4)
            def _(i):
                at = pl.ds(pl.multiple_of(i * chunk, 128), chunk)
                part = dot(gb[s, :, at], wb[s, at, :])
                if s == 0:
                    dacc[...] = jnp.where(i == 0, part, dacc[...] + part)
                else:
                    dacc[...] += part

        def weight_terms(s):
            @pl.loop(0, NZ)
            def _(i):
                at = pl.ds(pl.multiple_of(i * strip, 128), strip)
                part = lax.dot_general(gb[s, :, at], acat[...], TN, preferred_element_type=F32)
                pb[s, i] = (part * token_scale).astype(BF16).reshape(2, rows, pair)

        def core_terms(s):
            return remote(pb.at[s, :, 1 - c], rc.at[s], pc_s.at[s], pc_r.at[s], core_peer)

        ring = {}

        def ring_value(s, d, k, zd):
            dc = pl.ds(d * cols, cols)
            value = pb[s, zd, c, :, dc].astype(F32) + rc[s, zd, :, dc].astype(F32)
            if k > 0:
                value = value + rr[s, d, k - 1].astype(F32)
            return value

        def ring_send(s, k):
            for d in range(2):
                if k > 0:
                    ring[s, d, k - 1].wait_recv()
                zd = (z - 1 - k + NZ) % NZ if d == 0 else (z + 1 + k) % NZ
                dc = pl.ds(d * cols, cols)
                value = ring_value(s, d, k, zd).astype(BF16)
                rc[s, zd, :, dc] = value
                ring[s, d, k] = remote(
                    rc.at[s, zd, :, dc], rr.at[s, d, k], rr_s.at[s, d, k], rr_r.at[s, d, k],
                    z_peer(1 if d == 0 else -1),
                )

        def ring_last(s):
            for d in range(2):
                ring[s, d, NZ - 2].wait_recv()
                fx[s, d] = ring_value(s, d, NZ - 1, z).astype(BF16)

        def wait_g(s):
            for dy in (1, 3, 2):
                for zz in range(NZ):
                    g[s, dy, zz].wait_recv()

        wait_g(0)
        weight_terms(0)
        pc = [core_terms(0)]
        project(0)
        pc[0].wait_recv()
        for k in range(4):
            ring_send(0, k)
        wait_g(1)
        project(1)
        dob[mine, :] = dacc[:, col(xl, cols)].astype(BF16)
        dsend[...] = dacc[:, col(1 - xl, cols)].astype(BF16)
        d_copy = remote(dsend, dob.at[mine, :], ex_s.at[1], ex_r.at[1], x_partner)
        weight_terms(1)
        pc.append(core_terms(1))
        ring_send(0, 4)
        pc[1].wait_recv()
        ring_send(1, 0)
        d_copy.wait_recv()

        grads = []

        def backward(h):
            hc = pl.ds(h * HEAD_DIM, HEAD_DIM)

            @pl.loop(0, blocks)
            def _(i):
                at = pl.ds(pl.multiple_of(i * block, block), block)
                rows_d = dob[at, hc]
                d_probs = lax.dot_general(vb[:, hc], rows_d, NT, preferred_element_type=F32)
                delta = jnp.sum(
                    jnp.transpose(rows_d.astype(F32)) * ot[h, :, at].astype(F32),
                    axis=0, keepdims=True,
                )
                low = (pt[h, :, at].astype(F32) * (d_probs - delta)).astype(BF16)
                dsb[:, at] = low
                dqb[at, hc] = jnp.transpose(dot(kt[h], low) * inverse_root).astype(BF16)

            @pl.loop(0, blocks)
            def _(i):
                at = pl.ds(pl.multiple_of(i * block, block), block)
                dvb[at, hc] = dot(pt[h, at, :], dob[:, hc]).astype(BF16)
                dkb[at, hc] = (dot(dsb[at, :], qb[:, hc]) * inverse_root).astype(BF16)

            out_cols = pl.ds(pl.multiple_of(seq * cols + h * HEAD_DIM, 128), HEAD_DIM)
            for t, (src, dst) in enumerate(((dqb, dq_out), (dkb, dk_out), (dvb, dv_out))):
                for i, (dy, b) in enumerate(seq_offsets):
                    token_rows = ((xl + b) % 2) * half + ((y + dy) % NY) * tokens
                    grads.append(
                        remote(
                            src.at[pl.ds(pl.multiple_of(token_rows, 128), tokens), hc],
                            dst.at[:, out_cols],
                            gr_s.at[h, i, t], gr_r.at[h, i, t], seq_peer(dy, b),
                        )
                    )
                copy = pltpu.make_async_copy(
                    src.at[own_rows, hc], dst.at[:, out_cols], loc.at[20 + h * 3 + t]
                )
                copy.start()
                grads.append(copy)

        backward(0)
        ring_send(0, 5)
        ring_send(1, 1)
        backward(1)
        ring_send(0, 6)
        ring_send(1, 2)
        backward(2)
        ring_last(0)
        for k in range(3, NZ - 1):
            ring_send(1, k)
        ring_last(1)

        xs = [
            remote(
                fx.at[(xh + a) % 2, (xl + b) % 2], xr.at[i], x_s.at[i], x_r.at[i], x_peer(a, b)
            )
            for i, (a, b) in enumerate(x_offsets)
        ]
        for copy in xs:
            copy.wait_recv()
        total = fx[xh, xl].astype(F32)
        for i in range(3):
            total = total + xr[i].astype(F32)
        wg_out[...] = total

        for copy in grads:
            copy.wait()
        for copy in wx + qkv + wc + list(wz.values()) + list(g.values()) + pc + list(ring.values()):
            copy.wait_send()
        for copy in xs + [att_copy, d_copy]:
            copy.wait_send()

    any_space = pl.BlockSpec(memory_space=pl.ANY)
    dma = pltpu.SemaphoreType.DMA
    vmem = pltpu.VMEM
    scratch = [
        vmem((2, half, deep), BF16), vmem((2, deep, pair), BF16),
        vmem((length, cols), BF16), vmem((length, cols), BF16), vmem((length, cols), BF16),
        vmem((heads, length, length), BF16), vmem((length, length), BF16),
        vmem((heads, HEAD_DIM, length), BF16), vmem((heads, HEAD_DIM, length), BF16),
        vmem((heads, HEAD_DIM, length), BF16),
        vmem((length, cols), BF16), vmem((half, pair), BF16), vmem((length, cols), BF16),
        vmem((half, cols), BF16), vmem((half, pair), F32),
        vmem((2, NZ, 2, rows, pair), BF16), vmem((2, NZ, rows, pair), BF16),
        vmem((2, 2, NZ - 1, rows, cols), BF16), vmem((2, 2, rows, cols), BF16),
        vmem((3, rows, cols), BF16),
        vmem((length, cols), BF16), vmem((length, cols), BF16), vmem((length, cols), BF16),
        dma((32,)), dma((3,)), dma((3,)), dma((2, 2, 4)), dma((2, 2, 4)), dma((2, 8)), dma((2, 8)),
        dma((7, 3)), dma((7, 3)), dma((2, 3, NZ)), dma((2, 3, NZ)),
        dma((2,)), dma((2,)), dma((2,)), dma((2,)),
        dma((2, 2, NZ - 1)), dma((2, 2, NZ - 1)), dma((3,)), dma((3,)),
        dma((heads, 7, 3)), dma((heads, 7, 3)),
    ]
    out = jax.ShapeDtypeStruct((tokens, wide), BF16)
    return pl.pallas_call(
        kernel,
        name="joint_backward",
        out_shape=(out, out, out, jax.ShapeDtypeStruct((rows, cols), F32)),
        in_specs=[any_space] * 5,
        out_specs=(any_space, any_space, any_space, pl.BlockSpec(memory_space=pltpu.VMEM)),
        scratch_shapes=scratch,
        compiler_params=pltpu.CompilerParams(
            collective_id=0, has_side_effects=True, vmem_limit_bytes=60 * 2**20
        ),
    )


def shards(grad_out, queries, keys, values, out_weight):
    _, tokens, model = grad_out.shape
    rows, cols = out_weight.shape
    call = make_kernel(tokens, model, queries.shape[2], rows, cols, lax.axis_size("dp"))
    dq, dk, dv, wg = call(grad_out[0], queries[0], keys[0], values[0], out_weight)
    return (dq[None], dk[None], dv[None], wg)


def solution(mesh):
    in_specs = (
        P("dp", "seq", None),
        P("dp", "seq", None),
        P("dp", "seq", None),
        P("dp", "seq", None),
        P("dp", "seq"),
    )
    out_specs = (P("dp", "seq", None), P("dp", "seq", None), P("dp", "seq", None), P("dp", "seq"))
    return jax.shard_map(shards, mesh=mesh, in_specs=in_specs, out_specs=out_specs, check_vma=False)
```

time: 589 us -> 199 us (0.34); the launches traced: 577 us -> 198 us
  waiting for transfers between devices: 308 us -> 0 us
  Pallas kernels: 0 us -> 193 us
  local copies, waits for them, and re-layouts: 99.6 us -> 4.66 us
  other arithmetic: 75.8 us -> 0 us
  matrix products: 45.4 us -> 0 us
  starting transfers between devices: 33.4 us -> 0 us
  between operations: 14.4 us -> 0.66 us
    all_gather x2 -> x0, waiting for transfers between devices: 230 us -> none  [the longest x1 230 us: shards(): gathered = lax.all_gather(grad_out, 'seq', axis=1, tiled=True)[0]]
    pallas_call x0 -> x1, Pallas kernels: none -> 193 us  [shards(): call(grad_out[0], queries[0], keys[0], values[0], out_weight)]
    unnamed x8 -> x0, other arithmetic: 67.5 us -> none
    unnamed x4 -> x0, waiting for transfers between devices: 66.2 us -> none
    unnamed x36 -> x10, local copies, waits for them, and re-layouts: 67.8 us -> 4.66 us
    dot_general x12 -> x0, matrix products: 33.8 us -> none  [the longest x1 11.7 us: shards(): d_full = jnp.dot(gathered, whole_rows, preferred_element_type=jnp.float32)]
    all_to_all x6 -> x0, starting transfers between devices: 33.3 us -> none  [the longest x1 6.22 us: shards(): lax.all_to_all(keys, 'seq', split_axis=2, concat_axis=1, tiled=True)]
    all_to_all x6 -> x0, waiting for transfers between devices: 12.5 us -> none  [the longest x1 6.77 us: shards(): lax.all_to_all(query_local, 'seq', split_axis=1, concat_axis=2, tiled=True)]
  transfers between devices with their start and end apart: 9 -> 0, of which waited for: 5 -> 0; matrix products, arithmetic and copies ran while one was open for 25% -> 0% of each run, Pallas kernels for 0% -> 0%
where the time goes in v1:
time: 199 us; the launch traced here: 198 us
  Pallas kernels  193 us (97%)
  local copies, waits for them, and re-layouts  4.66 us (2%)
    pallas_call x1, Pallas kernels, shards(): call(grad_out[0], queries[0], keys[0], values[0], out_weight)  193 us
    unnamed x10, local copies, waits for them, and re-layouts  4.66 us

profile of v1, /device:TPU:6, one launch (start us, length us, event | category | flops | bytes accessed | tf_op | source)
XLA Modules:
  0.0 198.1 jit_solution(3907195157450955361)
XLA Ops:
  0.6 192.7 %joint_backward.1 = (bf16[128,3072]{1,0:T(8,128)(2,1)}, bf16[128,3072]{1,0:T(8,128)(2,1)}, bf16[128,3072]{1,0:T(8,128)(2,1)}, f32[192,384]{1,0:T(8,128)}) custom-call(bf16[128,6144]{1,0:T(8,128)(2,1)} %bitcast.7, bf16[128,3072]{1,0:T(8,128)(2,1)} %bitcast.11, bf16[128,3072]{1,0:T(8,128)(2,1)} %bitcast.12, bf16[128,3072]{1,0:T(8,128)(2,1)} %bitcast.13, ...), custom_call_target="tpu_custom_call" | custom-call | tf_op jit(solution)/shard_map/joint_backward/pallas_call | solution.py:388
  193.4 0.0 copy-start.1
  193.4 0.0 copy-start
  193.4 2.2 %copy.13 = bf16[1,128,3072]{2,1,0:T(8,128)(2,1)} copy(bf16[1,128,3072]{2,1,0:T(8,128)(2,1)} %bitcast.10) | data formatting | bytes 1572864
  195.6 0.0 copy-done.1
  195.6 0.0 copy-start.2
  195.6 0.9 copy.14
  196.5 0.0 copy-done
  196.5 0.9 copy.15
  197.3 0.0 copy-done.2
  197.3 0.7 copy.16
Async XLA Ops:
  193.4 2.2 %copy-start.1 = (bf16[128,3072]{1,0:T(8,128)(2,1)S(1)}, bf16[128,3072]{1,0:T(8,128)(2,1)}, u32[]{:S(2)}) copy-start(bf16[128,3072]{1,0:T(8,128)(2,1)} %get-tuple-element.9) | copy-start | bytes 2359300
  193.4 3.1 %copy-start = (bf16[128,3072]{1,0:T(8,128)(2,1)S(1)}, bf16[128,3072]{1,0:T(8,128)(2,1)}, u32[]{:S(2)}) copy-start(bf16[128,3072]{1,0:T(8,128)(2,1)} %get-tuple-element.10) | copy-start | bytes 2359300
  195.6 1.8 copy-start.2

commit v2 on v1

--- a/solution.py
+++ b/solution.py
@@ -121,57 +121,70 @@
                 )
         for copy in local:
             copy.wait()
-        for copy in wx:
-            copy.wait_recv()
 
         wz = {}
         wc = []
 
-        def w_block(s, zz, cc):
-            return wb.at[s, w_rows(zz, cc), :]
-
-        def w_core(s, zz, slot):
-            wc.append(
-                remote(w_block(s, zz, c), w_block(s, zz, c), wc_s.at[s, slot], wc_r.at[s, slot], core_peer)
-            )
-
-        def w_send(d, s, j):
+        flips = [(0, 0)] + x_offsets
+
+        def w_block(f, zz):
+            a, b = flips[f]
+            return wb.at[(xh + a) % 2, w_rows(zz, c), col((xl + b) % 2, cols)]
+
+        def w_core(f, zz, slot):
+            ref = w_block(f, zz)
+            wc.append(remote(ref, ref, wc_s.at[f, slot], wc_r.at[f, slot], core_peer))
+
+        def w_send(d, f, j):
             zz = (z - j + NZ) % NZ if d == 0 else (z + j) % NZ
-            ref = w_block(s, zz, c)
-            wz[d, s, j] = remote(ref, ref, wz_s.at[d, s, j], wz_r.at[d, s, j], z_peer(1 if d == 0 else -1))
-
-        def w_steps(d, s):
-            return 4 if d == s else 3
-
-        for s in range(2):
+            ref = w_block(f, zz)
+            wz[d, f, j] = remote(
+                ref, ref, wz_s.at[d, f, j], wz_r.at[d, f, j], z_peer(1 if d == 0 else -1)
+            )
+
+        def w_steps(d, f):
+            return 4 if d == f // 2 else 3
+
+        def w_step(j):
+            for f in range(4):
+                for d in range(2):
+                    if j < w_steps(d, f):
+                        wz[d, f, j].wait_recv()
+                        if j + 1 < w_steps(d, f):
+                            w_send(d, f, j + 1)
+                        zz = (z - 1 - j + NZ) % NZ if d == 0 else (z + 1 + j) % NZ
+                        w_core(f, zz, 1 + 2 * j + d if j < 3 else 7)
+
+        g = {}
+
+        def g_cols(i):
+            return pl.ds(i * (deep // 2), deep // 2)
+
+        def g_rows(dy):
+            return pl.ds(pl.multiple_of(((y + dy) % NY) * tokens, 128), tokens)
+
+        def g_copy(s, d, i, dy, slot):
+            ref = gb.at[s, g_rows(dy), g_cols(i)]
+            g[s, d, slot] = remote(
+                ref, ref, g_s.at[s, d, slot], g_r.at[s, d, slot], seq_peer(1 if d == 0 else 3, 0)
+            )
+
+        def g_send(s):
+            for slot in range(2):
+                for d in range(2):
+                    g_copy(s, d, slot ^ d, 0, slot)
+
+        def g_forward(s):
             for d in range(2):
-                w_send(d, s, 0)
-        for s in range(2):
-            w_core(s, z, 0)
-        for j in range(4):
-            for s in range(2):
+                g[s, d, 0].wait_recv()
+                g_copy(s, d, d, 3 if d == 0 else 1, 2)
+
+        def wait_g(s):
+            for slot in (1, 2):
                 for d in range(2):
-                    if j < w_steps(d, s):
-                        wz[d, s, j].wait_recv()
-                        if j + 1 < w_steps(d, s):
-                            w_send(d, s, j + 1)
-                        zz = (z - 1 - j + NZ) % NZ if d == 0 else (z + 1 + j) % NZ
-                        w_core(s, zz, 1 + 2 * j + d if j < 3 else 7)
-
-        g = {}
-        for s in range(2):
-            for dy in (1, 3, 2):
-                for zz in range(NZ):
-                    g[s, dy, zz] = remote(
-                        g_in.at[:, pl.ds((2 * zz + s) * strip, strip)],
-                        gb.at[s, y_rows, pl.ds(zz * strip, strip)],
-                        g_s.at[s, dy - 1, zz], g_r.at[s, dy - 1, zz], seq_peer(dy, 0),
-                    )
-
-        for copy in qkv:
-            copy.wait_recv()
-
-        for h in range(heads):
+                    g[s, d, slot].wait_recv()
+
+        def forward(h):
             hc = pl.ds(h * HEAD_DIM, HEAD_DIM)
             kt[h] = jnp.transpose(kb[:, hc].astype(F32)).astype(BF16)
             vt[h] = jnp.transpose(vb[:, hc].astype(F32)).astype(BF16)
@@ -189,17 +202,6 @@
                 ot[h, :, at] = out
                 att[at, hc] = jnp.transpose(out.astype(F32)).astype(BF16)
 
-        mine = pl.ds(pl.multiple_of(xl * half, 128), half)
-        theirs = pl.ds(pl.multiple_of((1 - xl) * half, 128), half)
-        x_partner = seq_peer(0, 1)
-        att_copy = remote(
-            att.at[theirs, :], acat.at[:, col(xl, cols)], ex_s.at[0], ex_r.at[0], x_partner
-        )
-        acat[:, col(xl, cols)] = att[mine, :]
-        att_copy.wait_recv()
-        for copy in wc:
-            copy.wait_recv()
-
         def project(s):
             chunk = deep // 4
 
@@ -223,59 +225,55 @@
             return remote(pb.at[s, :, 1 - c], rc.at[s], pc_s.at[s], pc_r.at[s], core_peer)
 
         ring = {}
-
-        def ring_value(s, d, k, zd):
-            dc = pl.ds(d * cols, cols)
-            value = pb[s, zd, c, :, dc].astype(F32) + rc[s, zd, :, dc].astype(F32)
-            if k > 0:
-                value = value + rr[s, d, k - 1].astype(F32)
-            return value
+        xs = []
+        for i, (a, b) in enumerate(x_offsets):
+            xs.append(
+                pltpu.make_async_remote_copy(
+                    src_ref=fx.at[(xh + a) % 2, (xl + b) % 2], dst_ref=xr.at[i],
+                    send_sem=x_s.at[i], recv_sem=x_r.at[i],
+                    device_id=x_peer(a, b), device_id_type=MESH,
+                )
+            )
+
+        def half_cols(q):
+            return pl.ds(q * cols, cols)
+
+        def own_terms(s, q, zd):
+            return pb[s, zd, c, :, half_cols(q)].astype(F32) + rc[s, zd, :, half_cols(q)].astype(F32)
 
         def ring_send(s, k):
-            for d in range(2):
-                if k > 0:
-                    ring[s, d, k - 1].wait_recv()
-                zd = (z - 1 - k + NZ) % NZ if d == 0 else (z + 1 + k) % NZ
-                dc = pl.ds(d * cols, cols)
-                value = ring_value(s, d, k, zd).astype(BF16)
-                rc[s, zd, :, dc] = value
-                ring[s, d, k] = remote(
-                    rc.at[s, zd, :, dc], rr.at[s, d, k], rr_s.at[s, d, k], rr_r.at[s, d, k],
-                    z_peer(1 if d == 0 else -1),
-                )
+            for side in (1, 0):
+                for d in range(2):
+                    if k == 0 and side:
+                        continue
+                    zd = (z + 4 - k) % NZ if d == 0 else (z + 4 + k) % NZ
+                    value = own_terms(s, d ^ side, zd)
+                    if k > side:
+                        ring[s, d, side, k - 1].wait_recv()
+                        value = value + rr[s, d, side, k - 1].astype(F32)
+                    ref = rc.at[s, zd, :, half_cols(d ^ side)]
+                    ref[...] = value.astype(BF16)
+                    ring[s, d, side, k] = remote(
+                        ref, rr.at[s, d, side, k], rr_s.at[s, d, side, k], rr_r.at[s, d, side, k],
+                        z_peer(1 if d == 0 else -1),
+                    )
 
         def ring_last(s):
-            for d in range(2):
-                ring[s, d, NZ - 2].wait_recv()
-                fx[s, d] = ring_value(s, d, NZ - 1, z).astype(BF16)
-
-        def wait_g(s):
-            for dy in (1, 3, 2):
-                for zz in range(NZ):
-                    g[s, dy, zz].wait_recv()
-
-        wait_g(0)
-        weight_terms(0)
-        pc = [core_terms(0)]
-        project(0)
-        pc[0].wait_recv()
-        for k in range(4):
-            ring_send(0, k)
-        wait_g(1)
-        project(1)
-        dob[mine, :] = dacc[:, col(xl, cols)].astype(BF16)
-        dsend[...] = dacc[:, col(1 - xl, cols)].astype(BF16)
-        d_copy = remote(dsend, dob.at[mine, :], ex_s.at[1], ex_r.at[1], x_partner)
-        weight_terms(1)
-        pc.append(core_terms(1))
-        ring_send(0, 4)
-        pc[1].wait_recv()
-        ring_send(1, 0)
-        d_copy.wait_recv()
+            for q in range(2):
+                value = own_terms(s, q, z)
+                for d in range(2):
+                    ring[s, d, d ^ q, 3].wait_recv()
+                    value = value + rr[s, d, d ^ q, 3].astype(F32)
+                fx[s, q] = value.astype(BF16)
+            for i, (a, b) in enumerate(x_offsets):
+
+                @pl.when((xh + a) % 2 == s)
+                def _():
+                    xs[i].start()
 
         grads = []
 
-        def backward(h):
+        def backward_scores(h):
             hc = pl.ds(h * HEAD_DIM, HEAD_DIM)
 
             @pl.loop(0, blocks)
@@ -291,14 +289,19 @@
                 dsb[:, at] = low
                 dqb[at, hc] = jnp.transpose(dot(kt[h], low) * inverse_root).astype(BF16)
 
+        def backward_sums(h, left, right, out, factor):
+            hc = pl.ds(h * HEAD_DIM, HEAD_DIM)
+
             @pl.loop(0, blocks)
             def _(i):
                 at = pl.ds(pl.multiple_of(i * block, block), block)
-                dvb[at, hc] = dot(pt[h, at, :], dob[:, hc]).astype(BF16)
-                dkb[at, hc] = (dot(dsb[at, :], qb[:, hc]) * inverse_root).astype(BF16)
-
+                out[at, hc] = (dot(left[at, :], right[:, hc]) * factor).astype(BF16)
+
+        def send_grads(h, which):
+            hc = pl.ds(h * HEAD_DIM, HEAD_DIM)
             out_cols = pl.ds(pl.multiple_of(seq * cols + h * HEAD_DIM, 128), HEAD_DIM)
-            for t, (src, dst) in enumerate(((dqb, dq_out), (dkb, dk_out), (dvb, dv_out))):
+            for t in which:
+                src, dst = ((dqb, dq_out), (dkb, dk_out), (dvb, dv_out))[t]
                 for i, (dy, b) in enumerate(seq_offsets):
                     token_rows = ((xl + b) % 2) * half + ((y + dy) % NY) * tokens
                     grads.append(
@@ -314,24 +317,90 @@
                 copy.start()
                 grads.append(copy)
 
-        backward(0)
-        ring_send(0, 5)
+        for d in range(2):
+            w_send(d, 0, 0)
+        w_core(0, z, 0)
+        for f in range(1, 4):
+            wx[f - 1].wait_recv()
+            for d in range(2):
+                w_send(d, f, 0)
+            w_core(f, z, 0)
+        w_step(0)
+        g_send(0)
+        w_step(1)
+        w_step(2)
+        g_forward(0)
+        g_send(1)
+        for copy in qkv:
+            copy.wait_recv()
+        forward(0)
+        w_step(3)
+        for h in range(1, heads):
+            forward(h)
+
+        mine = pl.ds(pl.multiple_of(xl * half, 128), half)
+        theirs = pl.ds(pl.multiple_of((1 - xl) * half, 128), half)
+        x_partner = seq_peer(0, 1)
+        att_copy = remote(
+            att.at[theirs, :], acat.at[:, col(xl, cols)], ex_s.at[0], ex_r.at[0], x_partner
+        )
+        acat[:, col(xl, cols)] = att[mine, :]
+        wait_g(0)
+        att_copy.wait_recv()
+        weight_terms(0)
+        pc = [core_terms(0)]
+        g_forward(1)
+        for copy in wc:
+            copy.wait_recv()
+        pc[0].wait_recv()
+        ring_send(0, 0)
+        ring_send(0, 1)
+        project(0)
+        ring_send(0, 2)
+        wait_g(1)
+        project(1)
+        d_copies = []
+        for h in range(heads):
+            hc = pl.ds(h * HEAD_DIM, HEAD_DIM)
+            dsend[:, hc] = dacc[:, col((1 - xl) * heads + h, HEAD_DIM)].astype(BF16)
+            d_copies.append(
+                remote(
+                    dsend.at[:, hc], dob.at[mine, hc], ex_s.at[1 + h], ex_r.at[1 + h], x_partner
+                )
+            )
+        dob[mine, :] = dacc[:, col(xl, cols)].astype(BF16)
+        ring_send(0, 3)
+        weight_terms(1)
+        pc.append(core_terms(1))
+        d_copies[0].wait_recv()
+        backward_sums(0, pt.at[0], dob, dvb, 1.0)
+        send_grads(0, (2,))
+        pc[1].wait_recv()
+        ring_send(1, 0)
+        ring_last(0)
+        backward_scores(0)
+        send_grads(0, (0,))
         ring_send(1, 1)
-        backward(1)
-        ring_send(0, 6)
+        backward_sums(0, dsb, qb, dkb, inverse_root)
+        send_grads(0, (1,))
+        d_copies[1].wait_recv()
+        backward_sums(1, pt.at[1], dob, dvb, 1.0)
+        send_grads(1, (2,))
+        backward_scores(1)
+        send_grads(1, (0,))
         ring_send(1, 2)
-        backward(2)
-        ring_last(0)
-        for k in range(3, NZ - 1):
-            ring_send(1, k)
+        backward_sums(1, dsb, qb, dkb, inverse_root)
+        send_grads(1, (1,))
+        d_copies[2].wait_recv()
+        backward_sums(2, pt.at[2], dob, dvb, 1.0)
+        send_grads(2, (2,))
+        ring_send(1, 3)
+        backward_scores(2)
+        send_grads(2, (0,))
+        backward_sums(2, dsb, qb, dkb, inverse_root)
+        send_grads(2, (1,))
         ring_last(1)
 
-        xs = [
-            remote(
-                fx.at[(xh + a) % 2, (xl + b) % 2], xr.at[i], x_s.at[i], x_r.at[i], x_peer(a, b)
-            )
-            for i, (a, b) in enumerate(x_offsets)
-        ]
         for copy in xs:
             copy.wait_recv()
         total = fx[xh, xl].astype(F32)
@@ -343,7 +412,7 @@
             copy.wait()
         for copy in wx + qkv + wc + list(wz.values()) + list(g.values()) + pc + list(ring.values()):
             copy.wait_send()
-        for copy in xs + [att_copy, d_copy]:
+        for copy in xs + [att_copy] + d_copies:
             copy.wait_send()
 
     any_space = pl.BlockSpec(memory_space=pl.ANY)
@@ -358,13 +427,13 @@
         vmem((length, cols), BF16), vmem((half, pair), BF16), vmem((length, cols), BF16),
         vmem((half, cols), BF16), vmem((half, pair), F32),
         vmem((2, NZ, 2, rows, pair), BF16), vmem((2, NZ, rows, pair), BF16),
-        vmem((2, 2, NZ - 1, rows, cols), BF16), vmem((2, 2, rows, cols), BF16),
+        vmem((2, 2, 2, 4, rows, cols), BF16), vmem((2, 2, rows, cols), BF16),
         vmem((3, rows, cols), BF16),
         vmem((length, cols), BF16), vmem((length, cols), BF16), vmem((length, cols), BF16),
-        dma((32,)), dma((3,)), dma((3,)), dma((2, 2, 4)), dma((2, 2, 4)), dma((2, 8)), dma((2, 8)),
-        dma((7, 3)), dma((7, 3)), dma((2, 3, NZ)), dma((2, 3, NZ)),
-        dma((2,)), dma((2,)), dma((2,)), dma((2,)),
-        dma((2, 2, NZ - 1)), dma((2, 2, NZ - 1)), dma((3,)), dma((3,)),
+        dma((32,)), dma((3,)), dma((3,)), dma((2, 4, 4)), dma((2, 4, 4)), dma((4, 8)), dma((4, 8)),
+        dma((7, 3)), dma((7, 3)), dma((2, 2, 3)), dma((2, 2, 3)),
+        dma((4,)), dma((4,)), dma((2,)), dma((2,)),
+        dma((2, 2, 2, 4)), dma((2, 2, 2, 4)), dma((3,)), dma((3,)),
         dma((heads, 7, 3)), dma((heads, 7, 3)),
     ]
     out = jax.ShapeDtypeStruct((tokens, wide), BF16)

time: 199 us -> 148 us (0.74)
  Pallas kernels: 193 us -> 142 us
    pallas_call x1, Pallas kernels: 193 us -> 142 us  [shards(): call(grad_out[0], queries[0], keys[0], values[0], out_weight)]
where the time goes in v2:
time: 148 us
  Pallas kernels  142 us (96%)
  local copies, waits for them, and re-layouts  4.66 us (3%)
    pallas_call x1, Pallas kernels, shards(): call(grad_out[0], queries[0], keys[0], values[0], out_weight)  142 us
    unnamed x10, local copies, waits for them, and re-layouts  4.66 us

profile of v2, /device:TPU:6, one launch (start us, length us, event | category | flops | bytes accessed | tf_op | source)
XLA Modules:
  0.0 147.8 jit_solution(1514029232139953733)
XLA Ops:
  0.6 142.5 %joint_backward.1 = (bf16[128,3072]{1,0:T(8,128)(2,1)}, bf16[128,3072]{1,0:T(8,128)(2,1)}, bf16[128,3072]{1,0:T(8,128)(2,1)}, f32[192,384]{1,0:T(8,128)}) custom-call(bf16[128,6144]{1,0:T(8,128)(2,1)} %bitcast.7, bf16[128,3072]{1,0:T(8,128)(2,1)} %bitcast.11, bf16[128,3072]{1,0:T(8,128)(2,1)} %bitcast.12, bf16[128,3072]{1,0:T(8,128)(2,1)} %bitcast.13, ...), custom_call_target="tpu_custom_call" | custom-call | tf_op jit(solution)/shard_map/joint_backward/pallas_call | solution.py:457
  143.1 0.0 copy-start.1
  143.1 0.0 copy-start
  143.1 2.2 %copy.13 = bf16[1,128,3072]{2,1,0:T(8,128)(2,1)} copy(bf16[1,128,3072]{2,1,0:T(8,128)(2,1)} %bitcast.10) | data formatting | bytes 1572864
  145.3 0.0 copy-done.1
  145.3 0.0 copy-start.2
  145.3 0.9 copy.14
  146.2 0.0 copy-done
  146.2 0.9 copy.15
  147.1 0.0 copy-done.2
  147.1 0.7 copy.16
Async XLA Ops:
  143.1 2.2 %copy-start.1 = (bf16[128,3072]{1,0:T(8,128)(2,1)S(1)}, bf16[128,3072]{1,0:T(8,128)(2,1)}, u32[]{:S(2)}) copy-start(bf16[128,3072]{1,0:T(8,128)(2,1)} %get-tuple-element.9) | copy-start | bytes 2359300
  143.1 3.1 %copy-start = (bf16[128,3072]{1,0:T(8,128)(2,1)S(1)}, bf16[128,3072]{1,0:T(8,128)(2,1)}, u32[]{:S(2)}) copy-start(bf16[128,3072]{1,0:T(8,128)(2,1)} %get-tuple-element.10) | copy-start | bytes 2359300
  145.3 1.8 %copy-start.2 = (f32[192,384]{1,0:T(8,128)S(1)}, f32[192,384]{1,0:T(8,128)}, u32[]{:S(2)}) copy-start(f32[192,384]{1,0:T(8,128)} %get-tuple-element.19) | copy-start | bytes 884740

commit v3 on v2

--- a/solution.py
+++ b/solution.py
@@ -36,7 +36,7 @@
     def kernel(
         g_in, q_in, k_in, v_in, w_in,
         dq_out, dk_out, dv_out, wg_out,
-        gb, wb, qb, kb, vb, pt, dsb, kt, vt, ot, att, acat, dob, dsend, dacc,
+        gb, gt, wb, qb, kb, vb, pt, dsb, kt, vt, ot, att, acat, dob, dsend, dacc,
         pb, rc, rr, fx, xr, dqb, dkb, dvb,
         loc, wx_s, wx_r, wz_s, wz_r, wc_s, wc_r, qkv_s, qkv_r, g_s, g_r,
         ex_s, ex_r, pc_s, pc_r, rr_s, rr_r, x_s, x_r, gr_s, gr_r,
@@ -179,8 +179,8 @@
                 g[s, d, 0].wait_recv()
                 g_copy(s, d, d, 3 if d == 0 else 1, 2)
 
-        def wait_g(s):
-            for slot in (1, 2):
+        def wait_g(s, *slots):
+            for slot in slots:
                 for d in range(2):
                     g[s, d, slot].wait_recv()
 
@@ -202,27 +202,46 @@
                 ot[h, :, at] = out
                 att[at, hc] = jnp.transpose(out.astype(F32)).astype(BF16)
 
-        def project(s):
+        def project():
             chunk = deep // 4
 
             @pl.loop(0, 4)
             def _(i):
                 at = pl.ds(pl.multiple_of(i * chunk, 128), chunk)
-                part = dot(gb[s, :, at], wb[s, at, :])
+                part = dot(gb[0, :, at], wb[0, at, :])
+                dacc[...] = jnp.where(i == 0, part, dacc[...] + part)
+
+        def project_rows(*offsets):
+            for dy in offsets:
+
+                @pl.loop(0, pair // block)
+                def _(i):
+                    at = pl.ds(pl.multiple_of(i * block, block), block)
+                    dacc[g_rows(dy), at] += dot(gb[1, g_rows(dy), :], wb[1, :, at])
+
+        def turn_rows(*offsets):
+            for dy in offsets:
+
+                @pl.loop(0, NZ)
+                def _(i):
+                    at = pl.ds(pl.multiple_of(i * strip, 128), strip)
+                    gt[at, g_rows(dy)] = jnp.transpose(gb[1, g_rows(dy), at])
+
+        pc = {}
+
+        def weight_terms(s, *offsets):
+            for offset in offsets:
+                zd = (z + offset) % NZ
+                at = pl.ds(pl.multiple_of(zd * strip, 128), strip)
                 if s == 0:
-                    dacc[...] = jnp.where(i == 0, part, dacc[...] + part)
+                    part = lax.dot_general(gb[0, :, at], acat[...], TN, preferred_element_type=F32)
                 else:
-                    dacc[...] += part
-
-        def weight_terms(s):
-            @pl.loop(0, NZ)
-            def _(i):
-                at = pl.ds(pl.multiple_of(i * strip, 128), strip)
-                part = lax.dot_general(gb[s, :, at], acat[...], TN, preferred_element_type=F32)
-                pb[s, i] = (part * token_scale).astype(BF16).reshape(2, rows, pair)
-
-        def core_terms(s):
-            return remote(pb.at[s, :, 1 - c], rc.at[s], pc_s.at[s], pc_r.at[s], core_peer)
+                    part = dot(gt[at, :], acat[...])
+                pb[s, zd] = (part * token_scale).astype(BF16).reshape(2, rows, pair)
+                pc[s, offset] = remote(
+                    pb.at[s, zd, 1 - c], rc.at[s, zd], pc_s.at[s, offset], pc_r.at[s, offset],
+                    core_peer,
+                )
 
         ring = {}
         xs = []
@@ -242,6 +261,8 @@
             return pb[s, zd, c, :, half_cols(q)].astype(F32) + rc[s, zd, :, half_cols(q)].astype(F32)
 
         def ring_send(s, k):
+            for offset in {4 - k, 4 + k}:
+                pc[s, offset].wait_recv()
             for side in (1, 0):
                 for d in range(2):
                     if k == 0 and side:
@@ -259,6 +280,7 @@
                     )
 
         def ring_last(s):
+            pc[s, 0].wait_recv()
             for q in range(2):
                 value = own_terms(s, q, z)
                 for d in range(2):
@@ -292,10 +314,7 @@
         def backward_sums(h, left, right, out, factor):
             hc = pl.ds(h * HEAD_DIM, HEAD_DIM)
 
-            @pl.loop(0, blocks)
-            def _(i):
-                at = pl.ds(pl.multiple_of(i * block, block), block)
-                out[at, hc] = (dot(left[at, :], right[:, hc]) * factor).astype(BF16)
+            out[:, hc] = (dot(left[...], right[:, hc]) * factor).astype(BF16)
 
         def send_grads(h, which):
             hc = pl.ds(h * HEAD_DIM, HEAD_DIM)
@@ -317,6 +336,7 @@
                 copy.start()
                 grads.append(copy)
 
+        g_send(0)
         for d in range(2):
             w_send(d, 0, 0)
         w_core(0, z, 0)
@@ -325,75 +345,93 @@
             for d in range(2):
                 w_send(d, f, 0)
             w_core(f, z, 0)
+        mine = pl.ds(pl.multiple_of(xl * half, 128), half)
+        theirs = pl.ds(pl.multiple_of((1 - xl) * half, 128), half)
+        x_partner = seq_peer(0, 1)
+        att_copies = []
+
+        def send_attended(h):
+            hc = pl.ds(h * HEAD_DIM, HEAD_DIM)
+            ac = col(xl * heads + h, HEAD_DIM)
+            att_copies.append(
+                remote(att.at[theirs, hc], acat.at[:, ac], ex_s.at[h], ex_r.at[h], x_partner)
+            )
+            acat[:, ac] = att[mine, hc]
+
+        d_copies = []
+
+        def send_d_attn():
+            for h in range(heads):
+                hc = pl.ds(h * HEAD_DIM, HEAD_DIM)
+                dsend[:, hc] = dacc[:, col((1 - xl) * heads + h, HEAD_DIM)].astype(BF16)
+                d_copies.append(
+                    remote(
+                        dsend.at[:, hc], dob.at[mine, hc],
+                        ex_s.at[heads + h], ex_r.at[heads + h], x_partner,
+                    )
+                )
+            dob[mine, :] = dacc[:, col(xl, cols)].astype(BF16)
+
         w_step(0)
-        g_send(0)
         w_step(1)
-        w_step(2)
         g_forward(0)
-        g_send(1)
         for copy in qkv:
             copy.wait_recv()
         forward(0)
+        send_attended(0)
+        w_step(2)
+        g_send(1)
+        forward(1)
+        send_attended(1)
+        forward(2)
+        send_attended(2)
+        wait_g(0, 1, 2)
+        for copy in att_copies:
+            copy.wait_recv()
+        weight_terms(0, 4, 3, 5)
+        ring_send(0, 0)
+        weight_terms(0, 2, 6, 1, 7, 0)
+        ring_send(0, 1)
+        g_forward(1)
         w_step(3)
-        for h in range(1, heads):
-            forward(h)
-
-        mine = pl.ds(pl.multiple_of(xl * half, 128), half)
-        theirs = pl.ds(pl.multiple_of((1 - xl) * half, 128), half)
-        x_partner = seq_peer(0, 1)
-        att_copy = remote(
-            att.at[theirs, :], acat.at[:, col(xl, cols)], ex_s.at[0], ex_r.at[0], x_partner
-        )
-        acat[:, col(xl, cols)] = att[mine, :]
-        wait_g(0)
-        att_copy.wait_recv()
-        weight_terms(0)
-        pc = [core_terms(0)]
-        g_forward(1)
         for copy in wc:
             copy.wait_recv()
-        pc[0].wait_recv()
-        ring_send(0, 0)
-        ring_send(0, 1)
-        project(0)
+        project()
+        turn_rows(0)
+        project_rows(0)
         ring_send(0, 2)
-        wait_g(1)
-        project(1)
-        d_copies = []
-        for h in range(heads):
-            hc = pl.ds(h * HEAD_DIM, HEAD_DIM)
-            dsend[:, hc] = dacc[:, col((1 - xl) * heads + h, HEAD_DIM)].astype(BF16)
-            d_copies.append(
-                remote(
-                    dsend.at[:, hc], dob.at[mine, hc], ex_s.at[1 + h], ex_r.at[1 + h], x_partner
-                )
-            )
-        dob[mine, :] = dacc[:, col(xl, cols)].astype(BF16)
+        wait_g(1, 1)
+        turn_rows(1, 3)
+        project_rows(1, 3)
+        wait_g(1, 2)
+        project_rows(2)
+        send_d_attn()
+        turn_rows(2)
+        weight_terms(1, 4, 3, 5)
         ring_send(0, 3)
-        weight_terms(1)
-        pc.append(core_terms(1))
+        ring_send(1, 0)
         d_copies[0].wait_recv()
         backward_sums(0, pt.at[0], dob, dvb, 1.0)
         send_grads(0, (2,))
-        pc[1].wait_recv()
-        ring_send(1, 0)
+        d_copies[1].wait_recv()
+        backward_sums(1, pt.at[1], dob, dvb, 1.0)
+        send_grads(1, (2,))
+        weight_terms(1, 2, 6)
+        d_copies[2].wait_recv()
+        backward_sums(2, pt.at[2], dob, dvb, 1.0)
+        send_grads(2, (2,))
+        ring_send(1, 1)
         ring_last(0)
         backward_scores(0)
         send_grads(0, (0,))
-        ring_send(1, 1)
+        weight_terms(1, 1, 7, 0)
         backward_sums(0, dsb, qb, dkb, inverse_root)
         send_grads(0, (1,))
-        d_copies[1].wait_recv()
-        backward_sums(1, pt.at[1], dob, dvb, 1.0)
-        send_grads(1, (2,))
+        ring_send(1, 2)
         backward_scores(1)
         send_grads(1, (0,))
-        ring_send(1, 2)
         backward_sums(1, dsb, qb, dkb, inverse_root)
         send_grads(1, (1,))
-        d_copies[2].wait_recv()
-        backward_sums(2, pt.at[2], dob, dvb, 1.0)
-        send_grads(2, (2,))
         ring_send(1, 3)
         backward_scores(2)
         send_grads(2, (0,))
@@ -410,16 +448,16 @@
 
         for copy in grads:
             copy.wait()
-        for copy in wx + qkv + wc + list(wz.values()) + list(g.values()) + pc + list(ring.values()):
+        for copy in wx + qkv + wc + list(wz.values()) + list(g.values()) + list(ring.values()):
             copy.wait_send()
-        for copy in xs + [att_copy] + d_copies:
+        for copy in xs + att_copies + d_copies + list(pc.values()):
             copy.wait_send()
 
     any_space = pl.BlockSpec(memory_space=pl.ANY)
     dma = pltpu.SemaphoreType.DMA
     vmem = pltpu.VMEM
     scratch = [
-        vmem((2, half, deep), BF16), vmem((2, deep, pair), BF16),
+        vmem((2, half, deep), BF16), vmem((deep, half), BF16), vmem((2, deep, pair), BF16),
         vmem((length, cols), BF16), vmem((length, cols), BF16), vmem((length, cols), BF16),
         vmem((heads, length, length), BF16), vmem((length, length), BF16),
         vmem((heads, HEAD_DIM, length), BF16), vmem((heads, HEAD_DIM, length), BF16),
@@ -432,7 +470,7 @@
         vmem((length, cols), BF16), vmem((length, cols), BF16), vmem((length, cols), BF16),
         dma((32,)), dma((3,)), dma((3,)), dma((2, 4, 4)), dma((2, 4, 4)), dma((4, 8)), dma((4, 8)),
         dma((7, 3)), dma((7, 3)), dma((2, 2, 3)), dma((2, 2, 3)),
-        dma((4,)), dma((4,)), dma((2,)), dma((2,)),
+        dma((2 * heads,)), dma((2 * heads,)), dma((2, NZ)), dma((2, NZ)),
         dma((2, 2, 2, 4)), dma((2, 2, 2, 4)), dma((3,)), dma((3,)),
         dma((heads, 7, 3)), dma((heads, 7, 3)),
     ]
@@ -450,11 +488,40 @@
     )
 
 
+def place(arrays):
+    count = len(arrays)
+
+    def kernel(*refs):
+        sources, targets, held = refs[:count], refs[count : 2 * count], refs[2 * count : 3 * count]
+        sems = refs[3 * count]
+        loads = [pltpu.make_async_copy(sources[i], held[i], sems.at[0, i]) for i in range(count)]
+        stores = [pltpu.make_async_copy(held[i], targets[i], sems.at[1, i]) for i in range(count)]
+        for copy in loads:
+            copy.start()
+        for load, store in zip(loads, stores):
+            load.wait()
+            store.start()
+        for copy in stores:
+            copy.wait()
+
+    any_space = pl.BlockSpec(memory_space=pl.ANY)
+    return pl.pallas_call(
+        kernel,
+        name="place",
+        out_shape=tuple(jax.ShapeDtypeStruct(a.shape, a.dtype) for a in arrays),
+        in_specs=[any_space] * count,
+        out_specs=(any_space,) * count,
+        scratch_shapes=[pltpu.VMEM(a.shape, a.dtype) for a in arrays]
+        + [pltpu.SemaphoreType.DMA((2, count))],
+    )(*arrays)
+
+
 def shards(grad_out, queries, keys, values, out_weight):
     _, tokens, model = grad_out.shape
     rows, cols = out_weight.shape
     call = make_kernel(tokens, model, queries.shape[2], rows, cols, lax.axis_size("dp"))
-    dq, dk, dv, wg = call(grad_out[0], queries[0], keys[0], values[0], out_weight)
+    results = call(grad_out[0], queries[0], keys[0], values[0], out_weight)
+    dq, dk, dv, wg = place(results)
     return (dq[None], dk[None], dv[None], wg)
 
 

time: 148 us -> 137 us (0.926)
  Pallas kernels: 142 us -> 136 us
  local copies, waits for them, and re-layouts: 4.66 us -> 0 us
    pallas_call x1 -> x2, Pallas kernels: 142 us -> 136 us  [the longest x1 133 us: shards(): results = call(grad_out[0], queries[0], keys[0], values[0], out_weight)]
    unnamed x10 -> x0, local copies, waits for them, and re-layouts: 4.66 us -> none
where the time goes in v3:
time: 137 us
  Pallas kernels  136 us (99%)
    pallas_call x1, Pallas kernels, shards(): results = call(grad_out[0], queries[0], keys[0], values[0], out_weight)  133 us

profile of v3, /device:TPU:6, one launch (start us, length us, event | category | flops | bytes accessed | tf_op | source)
XLA Modules:
  0.0 137.0 jit_solution(15716075707522360328)
XLA Ops:
  0.6 133.5 %joint_backward.1 = (bf16[128,3072]{1,0:T(8,128)(2,1)}, bf16[128,3072]{1,0:T(8,128)(2,1)}, bf16[128,3072]{1,0:T(8,128)(2,1)}, f32[192,384]{1,0:T(8,128)}) custom-call(bf16[128,6144]{1,0:T(8,128)(2,1)} %bitcast.7, bf16[128,3072]{1,0:T(8,128)(2,1)} %bitcast.8, bf16[128,3072]{1,0:T(8,128)(2,1)} %bitcast.9, bf16[128,3072]{1,0:T(8,128)(2,1)} %bitcast.10, ...), custom_call_target="tpu_custom_call" | custom-call | tf_op jit(solution)/shard_map/joint_backward/pallas_call | solution.py:523
  134.1 2.7 %place.1 = (bf16[128,3072]{1,0:T(8,128)(2,1)}, bf16[128,3072]{1,0:T(8,128)(2,1)}, bf16[128,3072]{1,0:T(8,128)(2,1)}, f32[192,384]{1,0:T(8,128)}) custom-call(bf16[128,3072]{1,0:T(8,128)(2,1)} %get-tuple-element.12.refs_0_, bf16[128,3072]{1,0:T(8,128)(2,1)} %get-tuple-element.13.refs_1_, bf16[128,3072]{1,0:T(8,128)(2,1)} %get-tuple-element.14.refs_2_, ...), custom_call_target="tpu_custom_call" | custom-call | tf_op jit(solution)/shard_map/place/pallas_call | solution.py:508

commit v4 on v3

--- a/solution.py
+++ b/solution.py
@@ -49,6 +49,9 @@
         def seq_peer(dy, b):
             return {"dp": dp, "seq": ((y + dy) % NY) * 2 + (xl + b) % 2}
 
+        def core_turn(dy):
+            return dy + c * (NY - 2 * dy)
+
         def x_peer(a, b):
             return {"dp": z * 4 + ((xh + a) % 2) * 2 + c, "seq": y * 2 + (xl + b) % 2}
 
@@ -111,7 +114,7 @@
         ]
         qkv = []
         for i, (dy, b) in enumerate(seq_offsets):
-            device = seq_peer(dy, b)
+            device = seq_peer(core_turn(dy), b)
             for t, (src, dst) in enumerate(((q_in, qb), (k_in, kb), (v_in, vb))):
                 qkv.append(
                     remote(
@@ -322,12 +325,12 @@
             for t in which:
                 src, dst = ((dqb, dq_out), (dkb, dk_out), (dvb, dv_out))[t]
                 for i, (dy, b) in enumerate(seq_offsets):
-                    token_rows = ((xl + b) % 2) * half + ((y + dy) % NY) * tokens
+                    token_rows = ((xl + b) % 2) * half + ((y + core_turn(dy)) % NY) * tokens
                     grads.append(
                         remote(
                             src.at[pl.ds(pl.multiple_of(token_rows, 128), tokens), hc],
                             dst.at[:, out_cols],
-                            gr_s.at[h, i, t], gr_r.at[h, i, t], seq_peer(dy, b),
+                            gr_s.at[h, i, t], gr_r.at[h, i, t], seq_peer(core_turn(dy), b),
                         )
                     )
                 copy = pltpu.make_async_copy(

time: 137 us -> 138 us (level)
  no operation moved by 1% of the time
where the time goes in v4:
time: 138 us
  Pallas kernels  137 us (99%)
    pallas_call x1, Pallas kernels, shards(): results = call(grad_out[0], queries[0], keys[0], values[0], out_weight)  134 us

profile of v4, /device:TPU:6, one launch (start us, length us, event | category | flops | bytes accessed | tf_op | source)
XLA Modules:
  0.0 137.8 jit_solution(12335148991515195552)
XLA Ops:
  0.6 134.4 %joint_backward.1 = (bf16[128,3072]{1,0:T(8,128)(2,1)}, bf16[128,3072]{1,0:T(8,128)(2,1)}, bf16[128,3072]{1,0:T(8,128)(2,1)}, f32[192,384]{1,0:T(8,128)}) custom-call(bf16[128,6144]{1,0:T(8,128)(2,1)} %bitcast.7, bf16[128,3072]{1,0:T(8,128)(2,1)} %bitcast.8, bf16[128,3072]{1,0:T(8,128)(2,1)} %bitcast.9, bf16[128,3072]{1,0:T(8,128)(2,1)} %bitcast.10, ...), custom_call_target="tpu_custom_call" | custom-call | tf_op jit(solution)/shard_map/joint_backward/pallas_call | solution.py:526
  135.0 2.7 %place.1 = (bf16[128,3072]{1,0:T(8,128)(2,1)}, bf16[128,3072]{1,0:T(8,128)(2,1)}, bf16[128,3072]{1,0:T(8,128)(2,1)}, f32[192,384]{1,0:T(8,128)}) custom-call(bf16[128,3072]{1,0:T(8,128)(2,1)} %get-tuple-element.12.refs_0_, bf16[128,3072]{1,0:T(8,128)(2,1)} %get-tuple-element.13.refs_1_, bf16[128,3072]{1,0:T(8,128)(2,1)} %get-tuple-element.14.refs_2_, ...), custom_call_target="tpu_custom_call" | custom-call | tf_op jit(solution)/shard_map/place/pallas_call | solution.py:511
